TPU v7x, 32 devices: a whole 2x2x4 slice. The times are simulated.
32 devices in a mesh: gx: 4 (over z), gy: 8 (over y, x, core).
Axes of the slice: x: 2, y: 2, z: 4, core: 2. Of those that a mesh axis runs over, the one named last changes fastest.
Arguments:
- offsets: float32 [2, 16, 32, 256], P(None, 'gx', 'gy'), may hold values from 0 to 1
- probes: float32 [16, 16, 32, 256], P(None, 'gx', 'gy'), may hold values from -6 to 6
- counts: int32 [16, 32], P('gx', 'gy'), may hold values from 1 to 256, as said below
Outputs:
- kernel_product: float32 [16, 16, 32, 256], P(None, 'gx', 'gy')
Inputs may be any that keep to these rules, and one draw needn't show every extreme that they name: `counts`: each draw has a leaf with all 256 slots used and a leaf with one slot used.
All inputs are finite; a program needn't handle non-finite values.
Results may differ from a plain program's by a relative error of at most 0.0001.
Values sent between devices are 32-bit elements; how exact they have to be, the bound alone decides.
A program may use at most 64 MiB of HBM per device.

v0:
```python
import functools
import math

import jax
import jax.numpy as jnp
import numpy as np
from jax import lax
from jax.experimental import pallas as pl
from jax.experimental.pallas import tpu as pltpu
from jax.sharding import PartitionSpec as P

ORDER = 8
NODES = ORDER * ORDER
ROOT_THREE = 1.7320508075688772
LENGTH_SCALE = 6.0
AMPLITUDE = 1.0 / 96.0
SHORT_AMPLITUDE = 1.0 / 16.0
NUGGET = 0.5
RATIO = 12
UNIT = ROOT_THREE / LENGTH_SCALE
HIGH = lax.Precision.HIGH
HIGHEST = lax.Precision.HIGHEST
ROWS = 24


def node_table():
    slots = np.arange(ORDER)
    return np.cos((2.0 * slots + 1.0) * (np.pi / (2.0 * ORDER)))


def series_at_nodes():
    powers = np.arange(ORDER)
    slots = np.arange(ORDER)
    table = np.cos(powers[:, None] * (2.0 * slots[None, :] + 1.0) * (np.pi / (2.0 * ORDER)))
    table = table * (2.0 / ORDER)
    table[0] = 1.0 / ORDER
    return table


def interpolation(coords):
    angles = np.arccos(np.clip(coords, -1.0, 1.0))
    series = np.cos(angles[:, None] * np.arange(ORDER))
    return series @ series_at_nodes()


def child_maps():
    nodes = node_table()
    result = []
    for child_x in range(2):
        for child_y in range(2):
            weight_x = interpolation((nodes - 1.0) / 2.0 + child_x)
            weight_y = interpolation((nodes - 1.0) / 2.0 + child_y)
            result.append(
                (weight_x[:, None, :, None] * weight_y[None, :, None, :]).reshape(NODES, NODES)
            )
    return np.stack(result).astype(np.float32)


def matern(dist_sq):
    safe = jnp.maximum(dist_sq, 1e-30)
    scaled = safe * lax.rsqrt(safe)
    decay = jnp.exp(-scaled)
    square = decay * decay
    fourth = square * square
    short = fourth * fourth * fourth
    return decay * (AMPLITUDE + AMPLITUDE * scaled) + short * (
        SHORT_AMPLITUDE + (RATIO * SHORT_AMPLITUDE) * scaled
    )


def split(value):
    high = value.astype(jnp.bfloat16)
    return high, (value - high.astype(jnp.float32)).astype(jnp.bfloat16)


def dot(a, b):
    return jnp.dot(a, b, preferred_element_type=jnp.float32)


def split_dot(a, b):
    a_high, a_low = split(a)
    b_high, b_low = split(b)
    return dot(a_high, b_high) + dot(a_high, b_low) + dot(a_low, b_high)


def leaf_weights(coords, table_ref):
    axes = []
    for axis in range(2):
        t = 2.0 * coords[axis : axis + 1] - 1.0
        terms = [jnp.ones_like(t), t]
        while len(terms) < ORDER:
            terms.append(2.0 * t * terms[-1] - terms[-2])
        total = table_ref[:, 0:1] * terms[0]
        for n in range(1, ORDER):
            total = total + table_ref[:, n : n + 1] * terms[n]
        axes.append(total)
    return jnp.concatenate([axes[0][m : m + 1] * axes[1] for m in range(ORDER)], axis=0)


def up_kernel(side, count_ref, table_ref, maps_ref, offsets_ref, probes_ref, record_ref, *level_refs):
    slots = offsets_ref.shape[2]
    probes = probes_ref.shape[0]
    lane = lax.broadcasted_iota(jnp.int32, (1, slots), 1)
    for leaf in range(side * side):
        count = count_ref[leaf]
        masked = jnp.where(lane < count, probes_ref[:, leaf, :], 0.0)
        coords = offsets_ref[:, leaf, :]
        record_ref[leaf, 0:probes, :] = masked
        record_ref[leaf, probes : probes + 2, :] = coords
        record_ref[leaf, probes + 2 : ROWS, :] = jnp.full(
            (ROWS - probes - 2, slots), count.astype(jnp.float32)
        )
        weights = leaf_weights(coords, table_ref)
        level_refs[0][leaf] = lax.dot_general(
            masked, weights, (((1,), (1,)), ((), ())), precision=HIGHEST,
            preferred_element_type=jnp.float32,
        )
    for level in range(1, len(level_refs)):
        boxes = side >> level
        for x in range(boxes):
            for y in range(boxes):
                total = None
                for child in range(4):
                    source = (2 * x + child // 2) * 2 * boxes + 2 * y + child % 2
                    term = jnp.dot(
                        level_refs[level - 1][source], maps_ref[child], precision=HIGHEST,
                        preferred_element_type=jnp.float32,
                    )
                    total = term if total is None else total + term
                level_refs[level][x * boxes + y] = total


def near_kernel(
    side, count_ref, table_ref, window_ref, local_ref, out_ref, column_ref, probe_ref, result_ref
):
    wide = side + 2
    slots = window_ref.shape[2]
    probes = out_ref.shape[0]
    lane = lax.broadcasted_iota(jnp.int32, (1, slots), 1)

    def prepare(cell, carry):
        column_ref[cell] = jnp.transpose(window_ref[cell, probes:ROWS, :]) * UNIT
        high, low = split(window_ref[cell, 0:probes, :])
        probe_ref[cell] = jnp.concatenate([high, low], axis=0)
        return carry

    lax.fori_loop(0, wide * wide, prepare, 0)

    def one_leaf(leaf, carry):
        i = leaf // side
        j = leaf % side
        center = (i + 1) * wide + j + 1
        coords = window_ref[center, probes : probes + 2, :]
        far = jnp.dot(
            local_ref[leaf], leaf_weights(coords, table_ref), precision=HIGHEST,
            preferred_element_type=jnp.float32,
        )
        scaled_x = coords[0:1] * UNIT
        scaled_y = coords[1:2] * UNIT

        def one_neighbour(n, total):
            a = n // 3
            b = n % 3
            cell = (i + a) * wide + j + b
            row_x = scaled_x - (a - 1).astype(jnp.float32) * UNIT
            row_y = scaled_y - (b - 1).astype(jnp.float32) * UNIT

            def rows(first, size):
                delta_x = row_x - column_ref[cell, first : first + size, 0:1]
                delta_y = row_y - column_ref[cell, first : first + size, 1:2]
                high, low = split(matern(delta_x * delta_x + delta_y * delta_y))
                both = dot(probe_ref[cell, :, first : first + size], high)
                return both[:probes] + both[probes:] + dot(
                    probe_ref[cell, :probes, first : first + size], low
                )

            return lax.cond(
                count_ref[cell] > slots // 2,
                lambda: total + rows(0, slots),
                lambda: lax.cond(
                    count_ref[cell] > 0, lambda: total + rows(0, slots // 2), lambda: total
                ),
            )

        near = lax.fori_loop(0, 9, one_neighbour, jnp.zeros((probes, slots), jnp.float32))
        value = near + far + NUGGET * window_ref[center, 0:probes, :]
        result_ref[leaf] = jnp.where(lane < count_ref[center], value, 0.0)
        return carry

    lax.fori_loop(0, side * side, one_leaf, 0)
    for leaf in range(side * side):
        out_ref[:, leaf, :] = result_ref[leaf]


def list_tables():
    nodes = node_table() / 2.0
    node_x = np.repeat(nodes, ORDER)
    node_y = np.tile(nodes, ORDER)
    source = np.zeros((6, 6, NODES, 8))
    for x in range(6):
        for y in range(6):
            source[x, y, :, 0] = x + node_x
            source[x, y, :, 1] = y + node_y
            source[x, y, :, 2] = x
            source[x, y, :, 3] = y
    target = np.zeros((8, 2, 2, NODES))
    for x in range(2):
        for y in range(2):
            target[0, x, y] = 2 + x + node_x
            target[1, x, y] = 2 + y + node_y
            target[2, x, y] = 2 + x
            target[3, x, y] = 2 + y
    return (
        source.reshape(36 * NODES, 8).astype(np.float32),
        target.reshape(8, 4 * NODES).astype(np.float32),
    )


def list_kernel(source_ref, target_ref, *refs):
    count = len(refs) // 2
    width = target_ref.shape[1]
    for level in range(count):
        scale = UNIT * 2.0**level
        sources_ref, out_ref = refs[level], refs[count + level]
        total = jnp.zeros(out_ref.shape, jnp.float32)
        for group in range(source_ref.shape[0] // width):
            rows = slice(group * width, (group + 1) * width)
            delta_x = (target_ref[0:1] - source_ref[rows, 0:1]) * scale
            delta_y = (target_ref[1:2] - source_ref[rows, 1:2]) * scale
            apart = jnp.maximum(
                jnp.abs(target_ref[2:3] - source_ref[rows, 2:3]),
                jnp.abs(target_ref[3:4] - source_ref[rows, 3:4]),
            )
            matrix = jnp.where(apart > 1.5, matern(delta_x * delta_x + delta_y * delta_y), 0.0)
            total = total + split_dot(sources_ref[:, rows], matrix)
        out_ref[...] = total


def extended(block, sides, width):
    for axis, dim in sides:
        count = lax.axis_size(axis)
        forward = [(i, i + 1) for i in range(count - 1)]
        backward = [(target, source) for source, target in forward]
        low = lax.ppermute(
            lax.slice_in_dim(block, block.shape[dim] - width, None, axis=dim), axis, forward
        )
        high = lax.ppermute(lax.slice_in_dim(block, 0, width, axis=dim), axis, backward)
        block = jnp.concatenate([low, block, high], axis=dim)
    return block


def upward(children, maps):
    half_x = children.shape[0] // 2
    half_y = children.shape[1] // 2
    grouped = children.reshape((half_x, 2, half_y, 2) + children.shape[2:])
    return jnp.einsum(
        "xyrq,ixjypr->ijpq", maps.reshape(2, 2, NODES, NODES), grouped, precision=HIGHEST
    )


def interact_top(box_grid, own_x, own_y, box_side):
    nodes = jnp.asarray(node_table() * (box_side / 2.0), jnp.float32)
    node_x = jnp.repeat(nodes, ORDER)
    node_y = jnp.tile(nodes, ORDER)
    shift_x = (jnp.arange(box_grid.shape[0], dtype=jnp.int32) - own_x).astype(jnp.float32)
    shift_y = (jnp.arange(box_grid.shape[1], dtype=jnp.int32) - own_y).astype(jnp.float32)
    delta_x = (node_x[:, None] - node_x[None, :] - shift_x[:, None, None] * box_side) * UNIT
    delta_y = (node_y[:, None] - node_y[None, :] - shift_y[:, None, None] * box_side) * UNIT
    matrices = matern((delta_x * delta_x)[:, None] + (delta_y * delta_y)[None])
    separated = jnp.maximum(jnp.abs(shift_x)[:, None], jnp.abs(shift_y)[None]) >= 2.0
    return jnp.einsum(
        "abqr,abpr->pq",
        jnp.where(separated[:, :, None, None], matrices, 0.0),
        box_grid,
        precision=HIGHEST,
    )


def flat_list(window):
    return jnp.transpose(window, (2, 0, 1, 3)).reshape(window.shape[2], -1)


def per_device(offsets, probes, counts):
    count_p, side, _, slots = probes.shape
    depth = side.bit_length() - 1
    top = depth + 2
    index_x = lax.axis_index("gx")
    index_y = lax.axis_index("gy")
    size_x = lax.axis_size("gx")
    size_y = lax.axis_size("gy")
    leaves = side * side
    table = jnp.asarray(series_at_nodes().T, jnp.float32)
    maps = jnp.asarray(child_maps())
    smem = pl.BlockSpec(memory_space=pltpu.SMEM)
    vmem = pl.BlockSpec(memory_space=pltpu.VMEM)
    levels = pl.pallas_call(
        functools.partial(up_kernel, side),
        out_shape=[jax.ShapeDtypeStruct((leaves, ROWS, slots), jnp.float32)]
        + [
            jax.ShapeDtypeStruct(((side >> level) ** 2, count_p, NODES), jnp.float32)
            for level in range(depth + 1)
        ],
        in_specs=[smem, vmem, vmem, vmem, vmem],
        out_specs=[vmem] * (depth + 2),
        name="up",
    )(
        counts.reshape(leaves),
        table,
        maps,
        offsets.reshape(2, leaves, slots),
        probes.reshape(count_p, leaves, slots),
    )
    record, levels = levels[0], levels[1:]
    window = extended(record.reshape(side, side, ROWS, slots), (("gx", 0), ("gy", 1)), 1)
    wide = side + 2
    window_counts = window[:, :, count_p + 2, 0].astype(jnp.int32).reshape(wide * wide)

    lists = []
    for level in range(depth):
        boxes = side >> level
        flat = levels[level].reshape(boxes, boxes, count_p * NODES)
        rim = extended(flat, (("gx", 0), ("gy", 1)), 2)
        rim = rim.reshape(boxes + 4, boxes + 4, count_p, NODES)
        lists.append(
            jnp.concatenate(
                [
                    flat_list(rim[2 * x : 2 * x + 6, 2 * y : 2 * y + 6])
                    for x in range(boxes // 2)
                    for y in range(boxes // 2)
                ],
                axis=0,
            )
        )
    gathered = lax.all_gather(
        levels[depth].reshape(1, count_p * NODES), ("gx", "gy"), axis=0, tiled=True
    )
    grids = [gathered.reshape(size_x, size_y, count_p, NODES)]
    for _ in range(top - depth):
        grids.append(upward(grids[-1], maps))
    for level in range(depth, top):
        shrink = 2 ** (level - depth)
        padded = jnp.pad(grids[level - depth], ((2, 2), (2, 2), (0, 0), (0, 0)))
        first_x = index_x // (2 * shrink) * 2
        first_y = index_y // (2 * shrink) * 2
        lists.append(
            flat_list(
                lax.dynamic_slice(padded, (first_x, first_y, 0, 0), (6, 6, count_p, NODES))
            )
        )
    source_table, target_table = list_tables()
    met = pl.pallas_call(
        list_kernel,
        out_shape=[
            jax.ShapeDtypeStruct((entry.shape[0], 4 * NODES), jnp.float32) for entry in lists
        ],
        in_specs=[vmem] * (2 + len(lists)),
        out_specs=[vmem] * len(lists),
        name="lists",
    )(jnp.asarray(source_table), jnp.asarray(target_table), *lists)

    if max(grids[-1].shape[:2]) > 2:
        local = interact_top(grids[-1], index_x // 2**(top - depth), index_y // 2**(top - depth), 2.0**top)
    else:
        local = jnp.zeros((count_p, NODES), jnp.float32)
    for level in range(top - 1, depth - 1, -1):
        shrink = 2 ** (level - depth)
        child = (index_x // shrink) % 2 * 2 + (index_y // shrink) % 2
        own_map = lax.dynamic_index_in_dim(maps, child, 0, keepdims=False)
        own = lax.dynamic_slice_in_dim(met[level], child * NODES, NODES, axis=1)
        local = own + jnp.einsum("rq,pq->pr", own_map, local, precision=HIGHEST)
    local = local[None, None]
    for level in range(depth - 1, -1, -1):
        half = local.shape[0]
        spread = jnp.einsum("crq,ijpq->ijpcr", maps, local, precision=HIGHEST)
        spread = spread + met[level].reshape(half, half, count_p, 4, NODES)
        spread = spread.reshape(half, half, count_p, 2, 2, NODES)
        local = jnp.transpose(spread, (0, 3, 1, 4, 2, 5)).reshape(
            2 * half, 2 * half, count_p, NODES
        )
    result = pl.pallas_call(
        functools.partial(near_kernel, side),
        out_shape=jax.ShapeDtypeStruct((count_p, leaves, slots), jnp.float32),
        in_specs=[smem, vmem, vmem, vmem],
        out_specs=vmem,
        scratch_shapes=[
            pltpu.VMEM((wide * wide, slots, 8), jnp.float32),
            pltpu.VMEM((wide * wide, 2 * count_p, slots), jnp.bfloat16),
            pltpu.VMEM((leaves, count_p, slots), jnp.float32),
        ],
        name="near",
    )(
        window_counts,
        table,
        window.reshape(wide * wide, ROWS, slots),
        local.reshape(leaves, count_p, NODES),
    )
    return result.reshape(count_p, side, side, slots)


def solution(mesh):
    placed = (P(None, "gx", "gy", None), P(None, "gx", "gy", None), P("gx", "gy"))
    return jax.shard_map(
        per_device, mesh=mesh, in_specs=placed, out_specs=P(None, "gx", "gy", None), check_vma=False
    )
```

profile of v0, /device:TPU:9, one launch (start us, length us, event | category | flops | bytes accessed | tf_op | source)
XLA Modules:
  0.0 188.4 jit_solution(422351924323114598)
XLA Ops:
  0.0 1.7 reshape.90.probes_ref
  1.7 1.4 reshape.89.offsets_ref
  3.1 1.3 reshape.88.count_ref
  4.4 3.4 %up.1 = (f32[16,24,256]{2,1,0:T(8,128)}, f32[16,16,64]{2,1,0:T(8,128)}, f32[4,16,64]{2,1,0:T(8,128)}, f32[1,16,64]{2,1,0:T(8,128)}) custom-call(s32[16]{0:T(128)} %reshape.88.count_ref, f32[8,8]{1,0:T(8,128)} %constant.116.clone.table_ref, f32[4,64,64]{2,1,0:T(8,128)} %constant.117.clone.maps_ref, f32[2,16,256]{2,1,0:T(8,128)} %reshape.89.offsets_ref, ...), custom_call_target="tpu_custom_call" | custom-call | tf_op jit(solution)/shard_map/up/pallas_call | solution.py:296
  7.8 0.9 reshape.99
  8.7 3.2 %collective-permute-start.8 = (f32[2,2,1024]{2,1,0:T(2,128)S(1)}, f32[2,2,1024]{2,1,0:T(2,128)S(1)}, u32[]{:S(2)}, u32[]{:S(2)}) collective-permute-start(f32[2,2,1024]{2,1,0:T(2,128)S(1)} %reshape.99), channel_id=1, source_target_pairs={{0,8},{8,16},{16,24},{1,9},{9,17},{17,25},{2,10},{10,18},{18,26},{... | collective-permute-start | bytes 49160 | tf_op jit(solution)/shard_map/ppermute | solution.py:244
  11.9 2.1 %collective-permute-start.9 = (f32[2,2,1024]{2,1,0:T(2,128)S(1)}, f32[2,2,1024]{2,1,0:T(2,128)S(1)}, u32[]{:S(2)}, u32[]{:S(2)}) collective-permute-start(f32[2,2,1024]{2,1,0:T(2,128)S(1)} %reshape.99), channel_id=1, source_target_pairs={{8,0},{16,8},{24,16},{9,1},{17,9},{25,17},{10,2},{18,10},{26,18},{... | collective-permute-start | bytes 49160 | tf_op jit(solution)/shard_map/ppermute | solution.py:247
  14.0 0.9 fusion.14
  15.0 3.2 %collective-permute-start.4 = (f32[2,4,1024]{2,1,0:T(4,128)S(1)}, f32[2,4,1024]{2,1,0:T(4,128)S(1)}, u32[]{:S(2)}, u32[]{:S(2)}) collective-permute-start(f32[2,4,1024]{2,1,0:T(4,128)S(1)} %slice.59), channel_id=1, source_target_pairs={{0,8},{8,16},{16,24},{1,9},{9,17},{17,25},{2,10},{10,18},{18,26},{... | collective-permute-start | bytes 98312 | tf_op jit(solution)/shard_map/ppermute | solution.py:244
  18.3 2.1 %collective-permute-start.5 = (f32[2,4,1024]{2,1,0:T(4,128)S(1)}, f32[2,4,1024]{2,1,0:T(4,128)S(1)}, u32[]{:S(2)}, u32[]{:S(2)}) collective-permute-start(f32[2,4,1024]{2,1,0:T(4,128)S(1)} %slice.61), channel_id=1, source_target_pairs={{8,0},{16,8},{24,16},{9,1},{17,9},{25,17},{10,2},{18,10},{26,18},{... | collective-permute-start | bytes 98312 | tf_op jit(solution)/shard_map/ppermute | solution.py:247
  20.3 1.0 slice_bitcast_fusion.5
  21.3 3.2 %collective-permute-start = (f32[1,4,24,256]{3,2,1,0:T(8,128)S(1)}, f32[1,4,24,256]{3,2,1,0:T(8,128)S(1)}, u32[]{:S(2)}, u32[]{:S(2)}) collective-permute-start(f32[1,4,24,256]{3,2,1,0:T(8,128)S(1)} %get-tuple-element.27), channel_id=1, source_target_pairs={{0,8},{8,16},{16,24},{1,9},{9,17},{17,25},{2,10},{10,18},{18,26},{... | collective-permute-start | bytes 294920 | tf_op jit(solution)/shard_map/ppermute | solution.py:244
  24.6 0.8 reshape.113
  25.3 35.4 %all-gather = f32[32,1,1024]{2,1,0:T(1,128)S(1)} all-gather(f32[1,1,1024]{2,1,0:T(1,128)S(1)} %reshape.113), channel_id=1, replica_groups=mesh['gx'=4,'gy'=8] {'gx','gy'}, dimensions={0}, use_global_device_ids=true | all-gather | bytes 135168 | tf_op jit(solution)/shard_map/all_gather | solution.py:334
  60.8 0.3 reduce.1
  61.3 0.4 convolution_bitcast_fusion
  61.8 0.1 copy-done.3
  62.3 0.8 reshape.104.refs_2_
  63.0 0.2 copy.39
  63.2 0.8 reshape.106.refs_3_
  64.0 8.5 %collective-permute-start.1 = (f32[1,4,24,256]{3,2,1,0:T(8,128)S(1)}, f32[1,4,24,256]{3,2,1,0:T(8,128)S(1)}, u32[]{:S(2)}, u32[]{:S(2)}) collective-permute-start(f32[1,4,24,256]{3,2,1,0:T(8,128)S(1)} %get-tuple-element.28), channel_id=1, source_target_pairs={{8,0},{16,8},{24,16},{9,1},{17,9},{25,17},{10,2},{18,10},{26,18},{... | collective-permute-start | bytes 294920 | tf_op jit(solution)/shard_map/ppermute | solution.py:247
  72.5 1.9 %collective-permute-start.10 = (f32[6,2,1024]{2,1,0:T(2,128)S(1)}, f32[6,2,1024]{2,1,0:T(2,128)S(1)}, u32[]{:S(2)}, u32[]{:S(2)}) collective-permute-start(f32[6,2,1024]{2,1,0:T(2,128)S(1)} %constant_dynamic-update-slice_fusion.3), channel_id=1, source_target_pairs={{0,1},{1,2},{2,3},{3,4},{4,5},{5,6},{6,7},{8,9},{9,10},{10,11},{11... | collective-permute-start | bytes 147464 | tf_op jit(solution)/shard_map/ppermute | solution.py:244
  74.5 2.4 %collective-permute-start.11 = (f32[6,2,1024]{2,1,0:T(2,128)S(1)}, f32[6,2,1024]{2,1,0:T(2,128)S(1)}, u32[]{:S(2)}, u32[]{:S(2)}) collective-permute-start(f32[6,2,1024]{2,1,0:T(2,128)S(1)} %constant_dynamic-update-slice_fusion.3), channel_id=1, source_target_pairs={{1,0},{2,1},{3,2},{4,3},{5,4},{6,5},{7,6},{9,8},{10,9},{11,10},{12... | collective-permute-start | bytes 147464 | tf_op jit(solution)/shard_map/ppermute | solution.py:247
  77.0 3.2 %collective-permute-start.6 = (f32[8,2,1024]{2,1,0:T(2,128)S(1)}, f32[8,2,1024]{2,1,0:T(2,128)S(1)}, u32[]{:S(2)}, u32[]{:S(2)}) collective-permute-start(f32[8,2,1024]{2,1,0:T(2,128)S(1)} %get-tuple-element.29), channel_id=1, source_target_pairs={{0,1},{1,2},{2,3},{3,4},{4,5},{5,6},{6,7},{8,9},{9,10},{10,11},{11... | collective-permute-start | bytes 196616 | tf_op jit(solution)/shard_map/ppermute | solution.py:244
  80.2 2.1 %collective-permute-start.7 = (f32[8,2,1024]{2,1,0:T(2,128)S(1)}, f32[8,2,1024]{2,1,0:T(2,128)S(1)}, u32[]{:S(2)}, u32[]{:S(2)}) collective-permute-start(f32[8,2,1024]{2,1,0:T(2,128)S(1)} %get-tuple-element.30), channel_id=1, source_target_pairs={{1,0},{2,1},{3,2},{4,3},{5,4},{6,5},{7,6},{9,8},{10,9},{11,10},{12... | collective-permute-start | bytes 196616 | tf_op jit(solution)/shard_map/ppermute | solution.py:247
  82.6 0.8 reshape.101.refs_1_
  83.4 2.4 %collective-permute-done.7 = f32[8,2,1024]{2,1,0:T(2,128)S(1)} collective-permute-done((f32[8,2,1024]{2,1,0:T(2,128)S(1)}, f32[8,2,1024]{2,1,0:T(2,128)S(1)}, u32[]{:S(2)}, u32[]{:S(2)}) %collective-permute-start.7) | collective-permute-done | bytes 65568 | tf_op jit(solution)/shard_map/ppermute | solution.py:247
  85.8 0.1 reshape.94
  86.0 0.1 slice_bitcast_fusion.3
  86.4 0.1 reshape.96
  86.7 0.1 reshape.97
  86.9 0.1 reshape.98
  87.0 0.9 pad_maximum_fusion.1.refs_0_
  87.9 14.6 %lists.1 = (f32[64,256]{1,0:T(8,128)}, f32[16,256]{1,0:T(8,128)}, f32[16,256]{1,0:T(8,128)}, f32[16,256]{1,0:T(8,128)}) custom-call(f32[2304,8]{1,0:T(8,128)} %constant.118.clone.source_ref, f32[8,256]{1,0:T(8,128)} %constant.119.clone.target_ref, f32[64,2304]{1,0:T(8,128)} %pad_maximum_fusion.1.refs_0_, f32[16,2304]{1,0:T(8,128)} %reshape.101.refs_1_, ...), custom_call_target="tpu_custom_call" | custom-call | tf_op jit(solution)/shard_map/lists/pallas_call | solution.py:351
  102.5 0.8 reshape.107
  103.4 0.8 convolution_add_fusion.3
  104.2 0.9 fusion
  105.1 0.4 convolution_add_fusion.1
  105.5 1.0 reshape.110
  106.6 1.9 %collective-permute-start.2 = (f32[6,1,24,256]{3,2,1,0:T(8,128)S(1)}, f32[6,1,24,256]{3,2,1,0:T(8,128)S(1)}, u32[]{:S(2)}, u32[]{:S(2)}) collective-permute-start(f32[6,1,24,256]{3,2,1,0:T(8,128)S(1)} %get-tuple-element.21), channel_id=1, source_target_pairs={{0,1},{1,2},{2,3},{3,4},{4,5},{5,6},{6,7},{8,9},{9,10},{10,11},{11... | collective-permute-start | bytes 442376 | tf_op jit(solution)/shard_map/ppermute | solution.py:244
  108.5 2.4 %collective-permute-start.3 = (f32[6,1,24,256]{3,2,1,0:T(8,128)S(1)}, f32[6,1,24,256]{3,2,1,0:T(8,128)S(1)}, u32[]{:S(2)}, u32[]{:S(2)}) collective-permute-start(f32[6,1,24,256]{3,2,1,0:T(8,128)S(1)} %get-tuple-element.22), channel_id=1, source_target_pairs={{1,0},{2,1},{3,2},{4,3},{5,4},{6,5},{7,6},{9,8},{10,9},{11,10},{12... | collective-permute-start | bytes 442376 | tf_op jit(solution)/shard_map/ppermute | solution.py:247
  110.9 0.5 convolution_add_fusion
  111.4 0.7 copy.42
  112.1 2.9 %collective-permute-done.3 = f32[6,1,24,256]{3,2,1,0:T(8,128)S(1)} collective-permute-done((f32[6,1,24,256]{3,2,1,0:T(8,128)S(1)}, f32[6,1,24,256]{3,2,1,0:T(8,128)S(1)}, u32[]{:S(2)}, u32[]{:S(2)}) %collective-permute-start.3) | collective-permute-done | bytes 147488 | tf_op jit(solution)/shard_map/ppermute | solution.py:247
  115.0 0.7 fusion.8
  115.8 0.6 convert_element_type.12.count_ref
  116.4 70.3 %near.1 = f32[16,16,256]{2,1,0:T(8,128)} custom-call(s32[36]{0:T(128)} %convert_element_type.12.count_ref, f32[8,8]{1,0:T(8,128)} %constant.116.clone.table_ref, f32[36,24,256]{2,1,0:T(8,128)} %bitcast.60, f32[16,16,64]{2,1,0:T(8,128)} %bitcast.64), custom_call_target="tpu_custom_call" | custom-call | tf_op jit(solution)/shard_map/near/pallas_call | solution.py:380
  186.7 1.7 reshape.112
  (48 shorter events, 1.8 us)
Async XLA Ops:
  7.8 53.5 %copy-start.4 = (f32[2,2,64,64,1,1]{3,2,1,5,4,0:T(8,128)S(1)}, f32[2,2,64,64,1,1]{3,2,1,5,4,0:T(8,128)}, u32[]{:S(2)}) copy-start(f32[2,2,64,64,1,1]{3,2,1,5,4,0:T(8,128)} %constant.128) | copy-start | bytes 196612
  8.7 55.3 %collective-permute-start.8 = (f32[2,2,1024]{2,1,0:T(2,128)S(1)}, f32[2,2,1024]{2,1,0:T(2,128)S(1)}, u32[]{:S(2)}, u32[]{:S(2)}) collective-permute-start(f32[2,2,1024]{2,1,0:T(2,128)S(1)} %reshape.99), channel_id=1, source_target_pairs={{0,8},{8,16},{16,24},{1,9},{9,17},{17,25},{2,10},{10,18},{18,26},{... | collective-permute-start | bytes 49160 | tf_op jit(solution)/shard_map/ppermute | solution.py:244
  11.9 60.6 %collective-permute-start.9 = (f32[2,2,1024]{2,1,0:T(2,128)S(1)}, f32[2,2,1024]{2,1,0:T(2,128)S(1)}, u32[]{:S(2)}, u32[]{:S(2)}) collective-permute-start(f32[2,2,1024]{2,1,0:T(2,128)S(1)} %reshape.99), channel_id=1, source_target_pairs={{8,0},{16,8},{24,16},{9,1},{17,9},{25,17},{10,2},{18,10},{26,18},{... | collective-permute-start | bytes 49160 | tf_op jit(solution)/shard_map/ppermute | solution.py:247
  15.0 59.5 %collective-permute-start.4 = (f32[2,4,1024]{2,1,0:T(4,128)S(1)}, f32[2,4,1024]{2,1,0:T(4,128)S(1)}, u32[]{:S(2)}, u32[]{:S(2)}) collective-permute-start(f32[2,4,1024]{2,1,0:T(4,128)S(1)} %slice.59), channel_id=1, source_target_pairs={{0,8},{8,16},{16,24},{1,9},{9,17},{17,25},{2,10},{10,18},{18,26},{... | collective-permute-start | bytes 98312 | tf_op jit(solution)/shard_map/ppermute | solution.py:244
  18.3 58.6 %collective-permute-start.5 = (f32[2,4,1024]{2,1,0:T(4,128)S(1)}, f32[2,4,1024]{2,1,0:T(4,128)S(1)}, u32[]{:S(2)}, u32[]{:S(2)}) collective-permute-start(f32[2,4,1024]{2,1,0:T(4,128)S(1)} %slice.61), channel_id=1, source_target_pairs={{8,0},{16,8},{24,16},{9,1},{17,9},{25,17},{10,2},{18,10},{26,18},{... | collective-permute-start | bytes 98312 | tf_op jit(solution)/shard_map/ppermute | solution.py:247
  21.3 85.2 %collective-permute-start = (f32[1,4,24,256]{3,2,1,0:T(8,128)S(1)}, f32[1,4,24,256]{3,2,1,0:T(8,128)S(1)}, u32[]{:S(2)}, u32[]{:S(2)}) collective-permute-start(f32[1,4,24,256]{3,2,1,0:T(8,128)S(1)} %get-tuple-element.27), channel_id=1, source_target_pairs={{0,8},{8,16},{16,24},{1,9},{9,17},{17,25},{2,10},{10,18},{18,26},{... | collective-permute-start | bytes 294920 | tf_op jit(solution)/shard_map/ppermute | solution.py:244
  61.1 0.9 copy-start.3
  64.0 42.5 %collective-permute-start.1 = (f32[1,4,24,256]{3,2,1,0:T(8,128)S(1)}, f32[1,4,24,256]{3,2,1,0:T(8,128)S(1)}, u32[]{:S(2)}, u32[]{:S(2)}) collective-permute-start(f32[1,4,24,256]{3,2,1,0:T(8,128)S(1)} %get-tuple-element.28), channel_id=1, source_target_pairs={{8,0},{16,8},{24,16},{9,1},{17,9},{25,17},{10,2},{18,10},{26,18},{... | collective-permute-start | bytes 294920 | tf_op jit(solution)/shard_map/ppermute | solution.py:247
  72.5 7.6 %collective-permute-start.10 = (f32[6,2,1024]{2,1,0:T(2,128)S(1)}, f32[6,2,1024]{2,1,0:T(2,128)S(1)}, u32[]{:S(2)}, u32[]{:S(2)}) collective-permute-start(f32[6,2,1024]{2,1,0:T(2,128)S(1)} %constant_dynamic-update-slice_fusion.3), channel_id=1, source_target_pairs={{0,1},{1,2},{2,3},{3,4},{4,5},{5,6},{6,7},{8,9},{9,10},{10,11},{11... | collective-permute-start | bytes 147464 | tf_op jit(solution)/shard_map/ppermute | solution.py:244
  74.5 7.8 %collective-permute-start.11 = (f32[6,2,1024]{2,1,0:T(2,128)S(1)}, f32[6,2,1024]{2,1,0:T(2,128)S(1)}, u32[]{:S(2)}, u32[]{:S(2)}) collective-permute-start(f32[6,2,1024]{2,1,0:T(2,128)S(1)} %constant_dynamic-update-slice_fusion.3), channel_id=1, source_target_pairs={{1,0},{2,1},{3,2},{4,3},{5,4},{6,5},{7,6},{9,8},{10,9},{11,10},{12... | collective-permute-start | bytes 147464 | tf_op jit(solution)/shard_map/ppermute | solution.py:247
  77.0 6.4 %collective-permute-start.6 = (f32[8,2,1024]{2,1,0:T(2,128)S(1)}, f32[8,2,1024]{2,1,0:T(2,128)S(1)}, u32[]{:S(2)}, u32[]{:S(2)}) collective-permute-start(f32[8,2,1024]{2,1,0:T(2,128)S(1)} %get-tuple-element.29), channel_id=1, source_target_pairs={{0,1},{1,2},{2,3},{3,4},{4,5},{5,6},{6,7},{8,9},{9,10},{10,11},{11... | collective-permute-start | bytes 196616 | tf_op jit(solution)/shard_map/ppermute | solution.py:244
  80.2 5.6 %collective-permute-start.7 = (f32[8,2,1024]{2,1,0:T(2,128)S(1)}, f32[8,2,1024]{2,1,0:T(2,128)S(1)}, u32[]{:S(2)}, u32[]{:S(2)}) collective-permute-start(f32[8,2,1024]{2,1,0:T(2,128)S(1)} %get-tuple-element.30), channel_id=1, source_target_pairs={{1,0},{2,1},{3,2},{4,3},{5,4},{6,5},{7,6},{9,8},{10,9},{11,10},{12... | collective-permute-start | bytes 196616 | tf_op jit(solution)/shard_map/ppermute | solution.py:247
  87.9 15.5 %copy-start.2 = (f32[4,64,64]{2,1,0:T(8,128)S(1)}, f32[4,64,64]{2,1,0:T(8,128)}, u32[]{:S(2)}) copy-start(f32[4,64,64]{2,1,0:T(8,128)} %constant.117.clone.maps_ref) | copy-start | bytes 196612
  87.9 18.6 %copy-start.1 = (f32[16,24,256]{2,1,0:T(8,128)S(1)}, f32[16,24,256]{2,1,0:T(8,128)}, u32[]{:S(2)}) copy-start(f32[16,24,256]{2,1,0:T(8,128)} %get-tuple-element.13) | copy-start | bytes 1179652
  102.5 8.4 %copy-start.5 = (f32[4,64,64,1,1]{2,1,0,4,3:T(8,128)S(1)}, f32[4,64,64,1,1]{2,1,0,4,3:T(8,128)}, u32[]{:S(2)}) copy-start(f32[4,64,64,1,1]{2,1,0,4,3:T(8,128)} %constant.129) | copy-start | bytes 196612
  106.6 5.5 %collective-permute-start.2 = (f32[6,1,24,256]{3,2,1,0:T(8,128)S(1)}, f32[6,1,24,256]{3,2,1,0:T(8,128)S(1)}, u32[]{:S(2)}, u32[]{:S(2)}) collective-permute-start(f32[6,1,24,256]{3,2,1,0:T(8,128)S(1)} %get-tuple-element.21), channel_id=1, source_target_pairs={{0,1},{1,2},{2,3},{3,4},{4,5},{5,6},{6,7},{8,9},{9,10},{10,11},{11... | collective-permute-start | bytes 442376 | tf_op jit(solution)/shard_map/ppermute | solution.py:244
  108.5 6.5 %collective-permute-start.3 = (f32[6,1,24,256]{3,2,1,0:T(8,128)S(1)}, f32[6,1,24,256]{3,2,1,0:T(8,128)S(1)}, u32[]{:S(2)}, u32[]{:S(2)}) collective-permute-start(f32[6,1,24,256]{3,2,1,0:T(8,128)S(1)} %get-tuple-element.22), channel_id=1, source_target_pairs={{1,0},{2,1},{3,2},{4,3},{5,4},{6,5},{7,6},{9,8},{10,9},{11,10},{12... | collective-permute-start | bytes 442376 | tf_op jit(solution)/shard_map/ppermute | solution.py:247
  115.0 1.4 copy-start
where the time goes:
time: 188 us
  Pallas kernels  88.3 us (47%)
  starting transfers between devices  36.1 us (19%)
  blocking collectives  35.4 us (19%)
  local copies, waits for them, and re-layouts  17.5 us (9%)
  waiting for transfers between devices  5.29 us (3%)
  matrix products  3.04 us (2%)
  other arithmetic  2.16 us (1%)
    pallas_call x1, Pallas kernels, per_device(): pl.pallas_call(functools.partial(near_kernel, side), out_shape=jax.ShapeD...  70.3 us
    all_gather x1, blocking collectives, per_device(): lax.all_gather(levels[depth].reshape(1, count_p * NODES), ('gx', 'gy'), a...  35.4 us
    ppermute x6, starting transfers between devices, extended(): lax.ppermute(lax.slice_in_dim(block, 0, width, axis=dim), axis, backward)  19.5 us
    ppermute x6, starting transfers between devices, extended(): lax.ppermute(lax.slice_in_dim(block, block.shape[dim] - width, None, axis...  16.6 us
    pallas_call x1, Pallas kernels, per_device(): pl.pallas_call(list_kernel, out_shape=[jax.ShapeDtypeStruct((entry.shape[...  14.6 us
    ppermute x6, waiting for transfers between devices, extended(): lax.ppermute(lax.slice_in_dim(block, 0, width, axis=dim), axis, backward)  5.27 us
  transfers between devices with their start and end apart: 12, of which 2 were waited for; matrix products, arithmetic and copies ran while one was open for 7% of the time, Pallas kernels for 8%

commit v1 on v0

v1 whole, which is shorter than its diff:
```python
import functools
import math

import jax
import jax.numpy as jnp
import numpy as np
from jax import lax
from jax.experimental import pallas as pl
from jax.experimental.pallas import tpu as pltpu
from jax.sharding import PartitionSpec as P

ORDER = 8
NODES = ORDER * ORDER
ROOT_THREE = 1.7320508075688772
LENGTH_SCALE = 6.0
AMPLITUDE = 1.0 / 96.0
SHORT_AMPLITUDE = 1.0 / 16.0
NUGGET = 0.5
RATIO = 12
UNIT = ROOT_THREE / LENGTH_SCALE
HIGH = lax.Precision.HIGH
HIGHEST = lax.Precision.HIGHEST
ROWS = 24


def node_table():
    slots = np.arange(ORDER)
    return np.cos((2.0 * slots + 1.0) * (np.pi / (2.0 * ORDER)))


def series_at_nodes():
    powers = np.arange(ORDER)
    slots = np.arange(ORDER)
    table = np.cos(powers[:, None] * (2.0 * slots[None, :] + 1.0) * (np.pi / (2.0 * ORDER)))
    table = table * (2.0 / ORDER)
    table[0] = 1.0 / ORDER
    return table


def interpolation(coords):
    angles = np.arccos(np.clip(coords, -1.0, 1.0))
    series = np.cos(angles[:, None] * np.arange(ORDER))
    return series @ series_at_nodes()


def child_maps():
    nodes = node_table()
    result = []
    for child_x in range(2):
        for child_y in range(2):
            weight_x = interpolation((nodes - 1.0) / 2.0 + child_x)
            weight_y = interpolation((nodes - 1.0) / 2.0 + child_y)
            result.append(
                (weight_x[:, None, :, None] * weight_y[None, :, None, :]).reshape(NODES, NODES)
            )
    return np.stack(result).astype(np.float32)


def matern(dist_sq):
    safe = jnp.maximum(dist_sq, 1e-30)
    scaled = safe * lax.rsqrt(safe)
    decay = jnp.exp(-scaled)
    square = decay * decay
    fourth = square * square
    short = fourth * fourth * fourth
    return decay * (AMPLITUDE + AMPLITUDE * scaled) + short * (
        SHORT_AMPLITUDE + (RATIO * SHORT_AMPLITUDE) * scaled
    )


def split(value):
    high = value.astype(jnp.bfloat16)
    return high, (value - high.astype(jnp.float32)).astype(jnp.bfloat16)


def dot(a, b):
    return jnp.dot(a, b, preferred_element_type=jnp.float32)


def split_dot(a, b):
    a_high, a_low = split(a)
    b_high, b_low = split(b)
    return dot(a_high, b_high) + dot(a_high, b_low) + dot(a_low, b_high)


def leaf_weights(coords, table_ref):
    axes = []
    for axis in range(2):
        t = 2.0 * coords[axis : axis + 1] - 1.0
        terms = [jnp.ones_like(t), t]
        while len(terms) < ORDER:
            terms.append(2.0 * t * terms[-1] - terms[-2])
        total = table_ref[:, 0:1] * terms[0]
        for n in range(1, ORDER):
            total = total + table_ref[:, n : n + 1] * terms[n]
        axes.append(total)
    return jnp.concatenate([axes[0][m : m + 1] * axes[1] for m in range(ORDER)], axis=0)


def up_kernel(side, count_ref, table_ref, maps_ref, offsets_ref, probes_ref, record_ref, *level_refs):
    slots = offsets_ref.shape[3]
    probes = probes_ref.shape[0]
    lane = lax.broadcasted_iota(jnp.int32, (1, slots), 1)
    for i in range(side):
        for j in range(side):
            count = count_ref[i, j]
            masked = jnp.where(lane < count, probes_ref[:, i, j, :], 0.0)
            coords = offsets_ref[:, i, j, :]
            record_ref[i, j, 0:probes, :] = masked
            record_ref[i, j, probes : probes + 2, :] = coords
            record_ref[i, j, probes + 2 : ROWS, :] = jnp.full(
                (ROWS - probes - 2, slots), count.astype(jnp.float32)
            )
            level_refs[0][i, j] = dot_rows(masked, leaf_weights(coords, table_ref))
    for level in range(1, len(level_refs)):
        boxes = side >> level
        for x in range(boxes):
            for y in range(boxes):
                level_refs[level][x, y] = merged(level_refs[level - 1], x, y, maps_ref)


def dot_rows(a, b):
    return lax.dot_general(
        a, b, (((1,), (1,)), ((), ())), precision=HIGHEST, preferred_element_type=jnp.float32
    )


def merged(children_ref, x, y, maps_ref, pad=0):
    total = None
    for child in range(4):
        term = jnp.dot(
            children_ref[pad + 2 * x + child // 2, pad + 2 * y + child % 2],
            maps_ref[child],
            precision=HIGHEST,
            preferred_element_type=jnp.float32,
        )
        total = term if total is None else total + term
    return total


def exchange_kernel(sizes, *refs):
    size_x, size_y = sizes
    sources, own_ref = refs[0:3], refs[3]
    windows, grid_ref = refs[4:7], refs[7]
    send_sem, recv_sem, line_send, line_recv, own_sem = refs[8:]
    ix = lax.axis_index("gx")
    iy = lax.axis_index("gy")
    steps = [(dx, dy) for dx in (-1, 0, 1) for dy in (-1, 0, 1) if (dx, dy) != (0, 0)]

    def inside(dx, dy):
        x = ix + dx
        y = iy + dy
        return (x >= 0) & (x < size_x) & (y >= 0) & (y < size_y)

    own_copy = pltpu.make_async_copy(own_ref.at[0, 0], grid_ref.at[ix, iy], own_sem)
    own_copy.start()
    for source, window in zip(sources, windows):
        side = source.shape[0]
        width = (window.shape[0] - side) // 2
        window[...] = jnp.zeros_like(window)
        window[width : width + side, width : width + side] = source[...]

    barrier = pltpu.get_barrier_semaphore()

    def greet(x, y):
        pl.semaphore_signal(
            barrier, inc=1, device_id=(x, y), device_id_type=pl.DeviceIdType.MESH
        )

    for k in range(1, size_x):
        greet(lax.rem(ix + k, size_x), iy)
    for k in range(1, size_y):
        greet(ix, lax.rem(iy + k, size_y))
    for dx, dy in steps:
        if dx and dy:
            pl.when(inside(dx, dy))(lambda dx=dx, dy=dy: greet(ix + dx, iy + dy))
    sides_x = jnp.minimum(ix, 1) + jnp.minimum(size_x - 1 - ix, 1)
    sides_y = jnp.minimum(iy, 1) + jnp.minimum(size_y - 1 - iy, 1)
    pl.semaphore_wait(barrier, size_x + size_y - 2 + sides_x * sides_y)

    def line_copy(slot, source, target, x, y):
        return pltpu.make_async_remote_copy(
            src_ref=source,
            dst_ref=target,
            send_sem=line_send.at[slot],
            recv_sem=line_recv.at[slot],
            device_id=(x, y),
            device_id_type=pl.DeviceIdType.MESH,
        )

    along_x = [
        line_copy(k - 1, own_ref.at[0, 0], grid_ref.at[ix, iy], lax.rem(ix + k, size_x), iy)
        for k in range(1, size_x)
    ]
    for copy in along_x:
        copy.start()

    def pieces(step, side, width):
        if step > 0:
            return pl.ds(side - width, width), pl.ds(0, width)
        if step < 0:
            return pl.ds(0, width), pl.ds(side + width, width)
        return pl.ds(0, side), pl.ds(width, side)

    def halo_copy(n, which):
        dx, dy = steps[n]
        source, window = sources[which], windows[which]
        side = source.shape[0]
        width = (window.shape[0] - side) // 2
        from_x, to_x = pieces(dx, side, width)
        from_y, to_y = pieces(dy, side, width)
        return pltpu.make_async_remote_copy(
            src_ref=source.at[from_x, from_y],
            dst_ref=window.at[to_x, to_y],
            send_sem=send_sem.at[which, n],
            recv_sem=recv_sem.at[which, n],
            device_id=(ix + dx, iy + dy),
            device_id_type=pl.DeviceIdType.MESH,
        )

    order = [(which, n) for which in range(3) for n in range(len(steps))]
    for which, n in order:
        pl.when(inside(*steps[n]))(lambda which=which, n=n: halo_copy(n, which).start())
    for copy in along_x:
        copy.wait_recv()
    own_copy.wait()
    along_y = [
        line_copy(
            size_x - 1 + k - 1, grid_ref.at[:, iy], grid_ref.at[:, iy],
            ix, lax.rem(iy + k, size_y),
        )
        for k in range(1, size_y)
    ]
    for copy in along_y:
        copy.start()
    for which, n in order:
        dx, dy = steps[n]
        pl.when(inside(-dx, -dy))(lambda which=which, n=n: halo_copy(n, which).wait_recv())
    for copy in along_y:
        copy.wait_recv()
    for which, n in order:
        pl.when(inside(*steps[n]))(lambda which=which, n=n: halo_copy(n, which).wait_send())
    for copy in along_x + along_y:
        copy.wait_send()


def near_kernel(
    side, count_ref, table_ref, window_ref, local_ref, out_ref, column_ref, probe_ref, result_ref
):
    wide = side + 2
    slots = window_ref.shape[3]
    probes = out_ref.shape[0]
    lane = lax.broadcasted_iota(jnp.int32, (1, slots), 1)

    def prepare(cell, carry):
        x = cell // wide
        y = cell % wide
        column_ref[cell] = jnp.transpose(window_ref[x, y, probes:ROWS, :]) * UNIT
        high, low = split(window_ref[x, y, 0:probes, :])
        probe_ref[cell] = jnp.concatenate([high, low], axis=0)
        return carry

    lax.fori_loop(0, wide * wide, prepare, 0)

    def one_leaf(leaf, carry):
        i = leaf // side
        j = leaf % side
        center = (i + 1) * wide + j + 1
        coords = window_ref[i + 1, j + 1, probes : probes + 2, :]
        far = jnp.dot(
            local_ref[i, j], leaf_weights(coords, table_ref), precision=HIGHEST,
            preferred_element_type=jnp.float32,
        )
        scaled_x = coords[0:1] * UNIT
        scaled_y = coords[1:2] * UNIT

        def one_neighbour(n, total):
            a = n // 3
            b = n % 3
            cell = (i + a) * wide + j + b
            row_x = scaled_x - (a - 1).astype(jnp.float32) * UNIT
            row_y = scaled_y - (b - 1).astype(jnp.float32) * UNIT

            def rows(first, size):
                delta_x = row_x - column_ref[cell, first : first + size, 0:1]
                delta_y = row_y - column_ref[cell, first : first + size, 1:2]
                high, low = split(matern(delta_x * delta_x + delta_y * delta_y))
                both = dot(probe_ref[cell, :, first : first + size], high)
                return both[:probes] + both[probes:] + dot(
                    probe_ref[cell, :probes, first : first + size], low
                )

            return lax.cond(
                count_ref[cell] > slots // 2,
                lambda: total + rows(0, slots),
                lambda: lax.cond(
                    count_ref[cell] > 0, lambda: total + rows(0, slots // 2), lambda: total
                ),
            )

        near = lax.fori_loop(0, 9, one_neighbour, jnp.zeros((probes, slots), jnp.float32))
        value = near + far + NUGGET * window_ref[i + 1, j + 1, 0:probes, :]
        result_ref[leaf] = jnp.where(lane < count_ref[center], value, 0.0)
        return carry

    lax.fori_loop(0, side * side, one_leaf, 0)
    for leaf in range(side * side):
        out_ref[:, leaf // side, leaf % side, :] = result_ref[leaf]


def list_tables():
    nodes = node_table() / 2.0
    node_x = np.repeat(nodes, ORDER)
    node_y = np.tile(nodes, ORDER)
    source = np.zeros((6, 6, NODES, 8))
    for x in range(6):
        for y in range(6):
            source[x, y, :, 0] = x + node_x
            source[x, y, :, 1] = y + node_y
            source[x, y, :, 2] = x
            source[x, y, :, 3] = y
    target = np.zeros((8, 2, 2, NODES))
    for x in range(2):
        for y in range(2):
            target[0, x, y] = 2 + x + node_x
            target[1, x, y] = 2 + y + node_y
            target[2, x, y] = 2 + x
            target[3, x, y] = 2 + y
    return (
        source.reshape(36 * NODES, 8).astype(np.float32),
        target.reshape(8, 4 * NODES).astype(np.float32),
    )


def matrices(target_ref, source_ref, rows, lanes, scale):
    delta_x = (target_ref[0:1, lanes] - source_ref[rows, 0:1]) * scale
    delta_y = (target_ref[1:2, lanes] - source_ref[rows, 1:2]) * scale
    apart = jnp.maximum(
        jnp.abs(target_ref[2:3, lanes] - source_ref[rows, 2:3]),
        jnp.abs(target_ref[3:4, lanes] - source_ref[rows, 3:4]),
    )
    return jnp.where(apart > 1.5, matern(delta_x * delta_x + delta_y * delta_y), 0.0)


def list_kernel(
    depth, extra, position_ref, source_ref, target_ref, far_target_ref, maps_ref, top_ref, *refs
):
    rims, grid_ref, out_ref = refs[:depth], refs[depth], refs[depth + 1]
    padded = refs[depth + 2 : depth + 2 + extra]
    locals_ref = refs[depth + 2 + extra :]
    probes = top_ref.shape[0]
    width = target_ref.shape[1]
    groups = source_ref.shape[0] // width
    per_group = width // NODES

    for level in range(extra):
        padded[level][...] = jnp.zeros_like(padded[level])
        count_x = padded[level].shape[0] - 4
        count_y = padded[level].shape[1] - 4
        if level == 0:
            padded[0][2 : 2 + count_x, 2 : 2 + count_y] = grid_ref[...]
        else:
            for x in range(count_x):
                for y in range(count_y):
                    padded[level][2 + x, 2 + y] = merged(padded[level - 1], x, y, maps_ref, 2)

    def gathered(load, group):
        boxes = [group * per_group + n for n in range(per_group)]
        return jnp.concatenate([load(box // 6, box % 6) for box in boxes], axis=1)

    ix = position_ref[0]
    iy = position_ref[1]
    own_child = []
    for level in range(extra):
        own_child.append((ix >> level) % 2 * 2 + (iy >> level) % 2)
    lanes = slice(0, extra * NODES)
    scales = far_target_ref[4:5, lanes]
    total = jnp.zeros((extra * probes, extra * NODES), jnp.float32)
    for group in range(groups):
        parts = []
        for level in range(extra):
            first_x = (ix >> (level + 1)) * 2
            first_y = (iy >> (level + 1)) * 2
            parts.append(
                gathered(lambda x, y: padded[level][first_x + x, first_y + y], group)
            )
        rows = slice(group * width, (group + 1) * width)
        matrix = matrices(far_target_ref, source_ref, rows, lanes, scales)
        total = total + split_dot(jnp.concatenate(parts, axis=0), matrix)
    local = top_ref[...]
    for level in range(extra - 1, -1, -1):
        own = total[level * probes : (level + 1) * probes, level * NODES : (level + 1) * NODES]
        local = own + dot_rows(local, maps_ref[own_child[level]])
    locals_ref[depth][0, 0] = local

    for level in range(depth - 1, -1, -1):
        rim_ref = rims[level]
        half = (rim_ref.shape[0] - 4) // 2
        total = jnp.zeros((half * half * probes, width), jnp.float32)
        for group in range(groups):
            parts = [
                gathered(lambda x, y: rim_ref[2 * px + x, 2 * py + y], group)
                for px in range(half)
                for py in range(half)
            ]
            rows = slice(group * width, (group + 1) * width)
            matrix = matrices(
                target_ref, source_ref, rows, slice(0, width), UNIT * 2.0**level
            )
            total = total + split_dot(jnp.concatenate(parts, axis=0), matrix)
        target = out_ref if level == 0 else locals_ref[level]
        above = jnp.concatenate(
            [locals_ref[level + 1][px, py] for px in range(half) for py in range(half)], axis=0
        )
        for child in range(4):
            value = total[:, child * NODES : (child + 1) * NODES] + dot_rows(
                above, maps_ref[child]
            )
            for box in range(half * half):
                target[2 * (box // half) + child // 2, 2 * (box % half) + child % 2] = value[
                    box * probes : (box + 1) * probes
                ]


def upward(children, maps):
    half_x = children.shape[0] // 2
    half_y = children.shape[1] // 2
    grouped = children.reshape((half_x, 2, half_y, 2) + children.shape[2:])
    return jnp.einsum(
        "xyrq,ixjypr->ijpq", maps.reshape(2, 2, NODES, NODES), grouped, precision=HIGHEST
    )


def interact_top(box_grid, own_x, own_y, box_side):
    nodes = jnp.asarray(node_table() * (box_side / 2.0), jnp.float32)
    node_x = jnp.repeat(nodes, ORDER)
    node_y = jnp.tile(nodes, ORDER)
    shift_x = (jnp.arange(box_grid.shape[0], dtype=jnp.int32) - own_x).astype(jnp.float32)
    shift_y = (jnp.arange(box_grid.shape[1], dtype=jnp.int32) - own_y).astype(jnp.float32)
    delta_x = (node_x[:, None] - node_x[None, :] - shift_x[:, None, None] * box_side) * UNIT
    delta_y = (node_y[:, None] - node_y[None, :] - shift_y[:, None, None] * box_side) * UNIT
    matrices = matern((delta_x * delta_x)[:, None] + (delta_y * delta_y)[None])
    separated = jnp.maximum(jnp.abs(shift_x)[:, None], jnp.abs(shift_y)[None]) >= 2.0
    return jnp.einsum(
        "abqr,abpr->pq",
        jnp.where(separated[:, :, None, None], matrices, 0.0),
        box_grid,
        precision=HIGHEST,
    )


def per_device(offsets, probes, counts):
    count_p, side, _, slots = probes.shape
    depth = side.bit_length() - 1
    extra = 2
    top = depth + extra
    index_x = lax.axis_index("gx")
    index_y = lax.axis_index("gy")
    size_x = lax.axis_size("gx")
    size_y = lax.axis_size("gy")
    wide = side + 2
    table = jnp.asarray(series_at_nodes().T, jnp.float32)
    maps = jnp.asarray(child_maps())
    smem = pl.BlockSpec(memory_space=pltpu.SMEM)
    vmem = pl.BlockSpec(memory_space=pltpu.VMEM)

    def shape(*dims):
        return jax.ShapeDtypeStruct(dims, jnp.float32)

    record, *levels = pl.pallas_call(
        functools.partial(up_kernel, side),
        out_shape=[shape(side, side, ROWS, slots)]
        + [shape(side >> k, side >> k, count_p, NODES) for k in range(depth + 1)],
        in_specs=[smem, vmem, vmem, vmem, vmem],
        out_specs=[vmem] * (depth + 2),
        name="up",
    )(counts, table, maps, offsets, probes)
    window, *rims, grid = pl.pallas_call(
        functools.partial(exchange_kernel, (size_x, size_y)),
        out_shape=[shape(wide, wide, ROWS, slots)]
        + [shape((side >> k) + 4, (side >> k) + 4, count_p, NODES) for k in range(depth)]
        + [shape(size_x, size_y, count_p, NODES)],
        in_specs=[vmem] * (depth + 2),
        out_specs=[vmem] * (depth + 2),
        scratch_shapes=[
            pltpu.SemaphoreType.DMA((depth + 1, 8)),
            pltpu.SemaphoreType.DMA((depth + 1, 8)),
            pltpu.SemaphoreType.DMA((size_x + size_y - 2,)),
            pltpu.SemaphoreType.DMA((size_x + size_y - 2,)),
            pltpu.SemaphoreType.DMA,
        ],
        compiler_params=pltpu.CompilerParams(collective_id=0, has_side_effects=True),
        name="exchange",
    )(record, *levels)

    if max(size_x, size_y) > 2 * 2**extra:
        grids = [grid]
        for _ in range(extra):
            grids.append(upward(grids[-1], maps))
        local = interact_top(grids[-1], index_x // 2**extra, index_y // 2**extra, 2.0**top)
    else:
        local = jnp.zeros((count_p, NODES), jnp.float32)
    source_table, target_table = list_tables()
    target_rows = jnp.asarray(target_table).reshape(8, 4, NODES)
    far_target = []
    for k in range(extra):
        child = (index_x >> k) % 2 * 2 + (index_y >> k) % 2
        rows = lax.dynamic_index_in_dim(target_rows, child, 1, keepdims=False)
        far_target.append(rows.at[4].set(UNIT * 2.0 ** (depth + k)))
    local = pl.pallas_call(
        functools.partial(list_kernel, depth, extra),
        out_shape=shape(side, side, count_p, NODES),
        in_specs=[smem] + [vmem] * (5 + depth + 1),
        out_specs=vmem,
        scratch_shapes=[
            pltpu.VMEM(((size_x >> k) + 4, (size_y >> k) + 4, count_p, NODES), jnp.float32)
            for k in range(extra)
        ]
        + [
            pltpu.VMEM((side >> k, side >> k, count_p, NODES), jnp.float32)
            for k in range(depth + 1)
        ],
        name="lists",
    )(
        jnp.stack([index_x, index_y]).astype(jnp.int32),
        jnp.asarray(source_table),
        jnp.asarray(target_table),
        jnp.concatenate(far_target, axis=1),
        maps,
        local,
        *rims,
        grid,
    )
    return pl.pallas_call(
        functools.partial(near_kernel, side),
        out_shape=shape(count_p, side, side, slots),
        in_specs=[smem, vmem, vmem, vmem],
        out_specs=vmem,
        scratch_shapes=[
            pltpu.VMEM((wide * wide, slots, 8), jnp.float32),
            pltpu.VMEM((wide * wide, 2 * count_p, slots), jnp.bfloat16),
            pltpu.VMEM((side * side, count_p, slots), jnp.float32),
        ],
        name="near",
    )(
        window[:, :, count_p + 2, 0].astype(jnp.int32).reshape(wide * wide),
        table,
        window,
        local,
    )


def solution(mesh):
    placed = (P(None, "gx", "gy", None), P(None, "gx", "gy", None), P("gx", "gy"))
    return jax.shard_map(
        per_device, mesh=mesh, in_specs=placed, out_specs=P(None, "gx", "gy", None), check_vma=False
    )
```

time: 188 us -> 108 us (0.57)
  starting transfers between devices: 36.1 us -> 0 us
  blocking collectives: 35.4 us -> 0 us
  local copies, waits for them, and re-layouts: 17.5 us -> 1.51 us
  Pallas kernels: 88.3 us -> 103 us
  waiting for transfers between devices: 5.29 us -> 0 us
  matrix products: 3.04 us -> 0 us
    ppermute x12 -> x0, starting transfers between devices: 36.1 us -> none  [the longest x6 19.5 us: extended(): lax.ppermute(lax.slice_in_dim(block, 0, width, axis=dim), axis, backward)]
    all_gather x1 -> x0, blocking collectives: 35.4 us -> none  [per_device(): lax.all_gather(levels[depth].reshape(1, count_p * NODES), ('gx', 'gy'), a...]
    pallas_call x3 -> x4, Pallas kernels: 88.3 us -> 103 us  [the longest x1 68.2 us: per_device(): pl.pallas_call(functools.partial(near_kernel, side), out_shape=shape(coun...]
    reshape x19 -> x0, local copies, waits for them, and re-layouts: 12.7 us -> none  [the longest x7 2.81 us: flat_list(): return jnp.transpose(window, (2, 0, 1, 3)).reshape(window.shape[2], -1)]
    ppermute x12 -> x0, waiting for transfers between devices: 5.29 us -> none  [the longest x6 5.27 us: extended(): lax.ppermute(lax.slice_in_dim(block, 0, width, axis=dim), axis, backward)]
    dot_general x5 -> x0, matrix products: 3.04 us -> none  [the longest x2 1.7 us: per_device(): local = own + jnp.einsum('rq,pq->pr', own_map, local, precision=HIGHEST)]
    slice x5 -> x0, local copies, waits for them, and re-layouts: 2.07 us -> none  [the longest x3 1.1 us: extended(): lax.slice_in_dim(block, block.shape[dim] - width, None, axis=dim)]
  transfers between devices with their start and end apart: 12 -> 0, of which waited for: 2 -> 0; matrix products, arithmetic and copies ran while one was open for 7% -> 0% of each run, Pallas kernels for 8% -> 0%
where the time goes in v1:
time: 108 us; the launch traced here: 107 us
  Pallas kernels  103 us (95%)
  other arithmetic  2.92 us (3%)
  local copies, waits for them, and re-layouts  1.51 us (1%)
    pallas_call x1, Pallas kernels, per_device(): pl.pallas_call(functools.partial(near_kernel, side), out_shape=shape(coun...  68.2 us
    pallas_call x1, Pallas kernels, per_device(): pl.pallas_call(functools.partial(exchange_kernel, (size_x, size_y)), out_...  19 us
    pallas_call x1, Pallas kernels, per_device(): pl.pallas_call(functools.partial(list_kernel, depth, extra), out_shape=sh...  11.9 us
    pallas_call x1, Pallas kernels, per_device(): pl.pallas_call(functools.partial(up_kernel, side), out_shape=[shape(side,...  3.43 us

profile of v1, /device:TPU:9, one launch (start us, length us, event | category | flops | bytes accessed | tf_op | source)
XLA Modules:
  0.0 107.0 jit_solution(15632645487652072106)
XLA Ops:
  0.0 0.0 copy-start
  0.0 3.4 %up.1 = (f32[4,4,24,256]{3,2,1,0:T(8,128)}, f32[4,4,16,64]{3,2,1,0:T(8,128)}, f32[2,2,16,64]{3,2,1,0:T(8,128)}, f32[1,1,16,64]{3,2,1,0:T(8,128)}) custom-call(s32[4,4]{1,0:T(4,128)} %count_ref.1, f32[8,8]{1,0:T(8,128)} %constant.139.clone.table_ref, f32[4,64,64]{2,1,0:T(8,128)} %constant.140.clone.maps_ref, f32[2,4,4,256]{3,2,1,0:T(4,128)} %offsets_ref.1, ...), custom_call_target="tpu_custom_call" | custom-call | tf_op jit(solution)/shard_map/up/pallas_call | solution.py:470
  3.4 19.0 %exchange.1 = (f32[6,6,24,256]{3,2,1,0:T(8,128)}, f32[8,8,16,64]{3,2,1,0:T(8,128)}, f32[6,6,16,64]{3,2,1,0:T(8,128)}, f32[4,8,16,64]{3,2,1,0:T(8,128)}) custom-call(f32[4,4,24,256]{3,2,1,0:T(8,128)} %get-tuple-element.37.refs_0_, f32[4,4,16,64]{3,2,1,0:T(8,128)} %get-tuple-element.38.refs_1_, f32[2,2,16,64]{3,2,1,0:T(8,128)} %get-tuple-element.39.refs_2_, ...), custom_call_target="tpu_custom_call" | custom-call | tf_op jit(solution)/shard_map/exchange/pallas_call | solution.py:478
  22.5 1.6 %convert_reduce_fusion = s32[6,6]{1,0:T(8,128)S(1)} fusion(f32[6,6,24,256]{3,2,1,0:T(8,128)} %get-tuple-element.41.window_ref), kind=kLoop, calls=%fused_computation | loop fusion | flops 36 | bytes 288 | tf_op jit(solution)/shard_map/convert_element_type | solution.py:546
  24.1 0.7 convert_element_type.8.count_ref
  24.8 0.6 pad_add_fusion.position_ref
  25.4 0.0 copy-done
  25.4 0.2 scatter.6
  25.7 0.7 pad_maximum_fusion.far_target_ref
  26.3 0.6 broadcast_in_dim.2.top_ref
  26.9 11.9 %lists.1.local_ref = f32[4,4,16,64]{3,2,1,0:T(8,128)} custom-call(s32[2]{0:T(128)} %pad_add_fusion.position_ref, f32[2304,8]{1,0:T(8,128)} %constant.142.clone.source_ref, f32[8,256]{1,0:T(8,128)} %constant.141.clone.target_ref, f32[8,128]{1,0:T(8,128)} %pad_maximum_fusion.far_target_ref, f32[4,64,64]{2,1,0:T(8,128)} %constant.140.clone.maps_ref, ...), custom_call_target="tpu_custom_call" | custom-call | tf_op jit(solution)/shard_map/lists/pallas_call | solution.py:510
  38.8 68.2 %near.1 = f32[16,4,4,256]{3,2,1,0:T(4,128)} custom-call(s32[36]{0:T(128)} %convert_element_type.8.count_ref, f32[8,8]{1,0:T(8,128)} %constant.139.clone.table_ref, f32[6,6,24,256]{3,2,1,0:T(8,128)} %get-tuple-element.41.window_ref, f32[4,4,16,64]{3,2,1,0:T(8,128)} %lists.1.local_ref), custom_call_target="tpu_custom_call" | custom-call | tf_op jit(solution)/shard_map/near/pallas_call | solution.py:534
  (4 shorter events, 0.0 us)
Async XLA Ops:
  0.0 25.4 %copy-start = (f32[8,4,64]{2,0,1:T(8,128)S(1)}, f32[8,4,64]{2,0,1:T(8,128)}, u32[]{:S(2)}) copy-start(f32[8,4,64]{2,0,1:T(8,128)} %constant.146) | copy-start | bytes 24580
